TPU v7x, 512 devices: a whole 4x4x16 slice. The times are simulated.
512 devices in a mesh: exp: 64 (over x, z), rep: 8 (over y, core).
Axes of the slice: x: 4, y: 4, z: 16, core: 2. Of those that a mesh axis runs over, the one named last changes fastest.
Arguments:
- latent: bfloat16 [128, 16, 64], P('exp'), may hold values from -6 to 6
- stem_weight: bfloat16 [144, 1536], replicated, may hold values from -0.5 to 0.5
- norm_gain: float32 [1536], replicated, may hold values from 0.4 to 1.6
- router_weight: bfloat16 [1536, 8], replicated, may hold values from -0.15625 to 0.15625
- routes: int32 [8192, 2], P('exp'), may hold values from 0 to 7, all different within a row; in each aligned block of 128 rows (0 to 127, 128 to 255, ...) at most 40 rows name the same one
- gate_weight: bfloat16 [1536, 24576], P('rep', 'exp'), may hold values from -0.15625 to 0.15625
- up_weight: bfloat16 [1536, 24576], P('rep', 'exp'), may hold values from -0.15625 to 0.15625
- down_weight: bfloat16 [24576, 1536], P('exp', 'rep'), may hold values from -0.109375 to 0.109375
- grad_mixed: bfloat16 [8192, 1536], P('exp'), may hold values from -6 to 6
Outputs:
- mixed: bfloat16 [8192, 1536], P('exp')
- grad_latent: float32 [128, 16, 64], P('exp')
- grad_gate: float32 [1536, 24576], P('rep', 'exp')
- grad_up: float32 [1536, 24576], P('rep', 'exp')
- grad_down: float32 [24576, 1536], P('exp', 'rep')
Inputs may be any that keep to these rules, and one draw needn't show every extreme that they name: `routes`: A token's 2 experts differ. Within the 128 tokens of one device, no expert is named more than 40 times, and in every draw some device's tokens name some expert exactly 40 times.
All inputs are finite; a program needn't handle non-finite values.
Results may differ from a plain program's by a relative error of at most 0.023.
Values may be sent and summed in bfloat16 or wider, within the bound.
A program may use at most 64 MiB of HBM per device.

v0:
```python
import jax
import jax.numpy as jnp
from jax import lax
from jax.sharding import PartitionSpec as P

CAP = 40


def with_halo(cells, sides, width):
    for axis, dim in sides:
        count = lax.axis_size(axis)
        ends = count - 1
        head = lax.slice_in_dim(cells, 0, width, axis=dim)
        tail = lax.slice_in_dim(cells, cells.shape[dim] - width, cells.shape[dim], axis=dim)
        cells = jnp.concatenate(
            [
                lax.ppermute(tail, axis, [(i, (i + 1) % count) for i in range(ends)]),
                cells,
                lax.ppermute(head, axis, [((i + 1) % count, i) for i in range(ends)]),
            ],
            axis=dim,
        )
    return cells


def rms_norm(values, gain):
    return values * lax.rsqrt(jnp.mean(values * values, axis=-1, keepdims=True) + 1e-06) * gain


def gating(picked):
    chosen = jax.nn.sigmoid(picked)
    return chosen / jnp.sum(chosen, axis=-1, keepdims=True)


def local(
    latent,
    stem_weight,
    norm_gain,
    router_weight,
    routes,
    gate_weight,
    up_weight,
    down_weight,
    grad_mixed,
):
    rows_here = latent.shape[0]
    channels = latent.shape[1]
    width = latent.shape[2]
    model_width = stem_weight.shape[1]
    experts = router_weight.shape[1]
    top_count = routes.shape[1]
    tok_here = rows_here * width
    shards = lax.axis_size("exp") // experts
    group_size = CAP // lax.axis_size("rep")
    slots = experts * CAP
    padded = with_halo(latent, (("exp", 0),), 1)
    padded = jnp.pad(padded, ((0, 0), (0, 0), (1, 1)))
    pieces = jnp.stack(
        [padded[i : i + rows_here, :, j : j + width] for i in range(3) for j in range(3)], axis=0
    )
    patches = jnp.transpose(pieces, (1, 3, 0, 2)).reshape(tok_here, 9 * channels)
    stem = jnp.dot(patches, stem_weight, preferred_element_type=jnp.float32).astype(jnp.bfloat16)
    stem_value = stem.astype(jnp.float32)
    normed = rms_norm(stem_value, norm_gain).astype(jnp.bfloat16)
    logits = jnp.dot(normed, router_weight, preferred_element_type=jnp.float32)
    picked = jnp.take_along_axis(logits, routes, axis=1)
    gates = gating(picked)
    upstream = grad_mixed.astype(jnp.float32)
    grad_rows = (
        (gates[:, :, None] * upstream[:, None, :]).astype(jnp.bfloat16).reshape(-1, model_width)
    )
    flat_routes = routes.reshape(-1)
    onehot = (flat_routes[:, None] == jnp.arange(experts, dtype=jnp.int32)[None, :]).astype(
        jnp.int32
    )
    position = jnp.sum(onehot * (jnp.cumsum(onehot, axis=0) - 1), axis=1)
    slot_index = flat_routes * CAP + position
    send_rows = (
        jnp.zeros((slots, model_width), jnp.bfloat16)
        .at[slot_index]
        .set(jnp.repeat(normed, top_count, axis=0))
    )
    send_grads = jnp.zeros((slots, model_width), jnp.bfloat16).at[slot_index].set(grad_rows)
    group_start = lax.axis_index("rep") * group_size
    group_rows = lax.dynamic_slice_in_dim(
        send_rows.reshape(experts, CAP, model_width), group_start, group_size, 1
    )
    group_grads = lax.dynamic_slice_in_dim(
        send_grads.reshape(experts, CAP, model_width), group_start, group_size, 1
    )
    fan_rows = jnp.repeat(group_rows, shards, axis=0)
    fan_grads = jnp.repeat(group_grads, shards, axis=0)
    gate_full, up_full = (
        lax.all_gather(gate_weight, "rep", axis=0, tiled=True),
        lax.all_gather(up_weight, "rep", axis=0, tiled=True),
    )
    down_full = lax.all_gather(down_weight, "rep", axis=1, tiled=True)
    hid_here = gate_full.shape[1]
    recv_rows = lax.all_to_all(fan_rows, "exp", split_axis=0, concat_axis=0, tiled=True)
    flat = recv_rows.reshape(-1, model_width)
    pre_gate = jnp.dot(flat, gate_full, preferred_element_type=jnp.float32)
    pre_up = jnp.dot(flat, up_full, preferred_element_type=jnp.float32)
    forward_hidden = (jax.nn.silu(pre_gate) * pre_up).astype(jnp.bfloat16)
    part = jnp.dot(forward_hidden, down_full, preferred_element_type=jnp.float32).astype(
        jnp.bfloat16
    )
    part, hidden, pre_gate, pre_up = (
        part.reshape(recv_rows.shape),
        forward_hidden,
        pre_gate,
        pre_up,
    )
    returned = lax.all_to_all(part, "exp", split_axis=0, concat_axis=0, tiled=True)
    recv_grads = lax.all_to_all(fan_grads, "exp", split_axis=0, concat_axis=0, tiled=True)
    flat = recv_grads.reshape(-1, model_width)
    grad_hidden = lax.dot_general(
        flat, down_full, (((1,), (1,)), ((), ())), preferred_element_type=jnp.float32
    )
    sigma = jax.nn.sigmoid(pre_gate)
    backward_grad_gate_pre = (
        grad_hidden * pre_up * sigma * (1.0 + pre_gate * (1.0 - sigma))
    ).astype(jnp.bfloat16)
    backward_grad_up_pre = (grad_hidden * pre_gate * sigma).astype(jnp.bfloat16)
    back = lax.dot_general(
        backward_grad_gate_pre,
        gate_full,
        (((1,), (1,)), ((), ())),
        preferred_element_type=jnp.float32,
    )
    back = back + lax.dot_general(
        backward_grad_up_pre, up_full, (((1,), (1,)), ((), ())), preferred_element_type=jnp.float32
    )
    back, grad_gate_pre, grad_up_pre = (
        back.astype(jnp.bfloat16).reshape(recv_grads.shape),
        backward_grad_gate_pre,
        backward_grad_up_pre,
    )
    returned_back = lax.all_to_all(back, "exp", split_axis=0, concat_axis=0, tiled=True)
    group_out = jnp.sum(
        returned.reshape(experts, shards, group_size, model_width).astype(jnp.float32), axis=1
    ).astype(jnp.bfloat16)
    group_back = jnp.sum(
        returned_back.reshape(experts, shards, group_size, model_width).astype(jnp.float32), axis=1
    ).astype(jnp.bfloat16)
    slot_out, slot_back = (
        lax.all_gather(group_out, "rep", axis=1, tiled=True),
        lax.all_gather(group_back, "rep", axis=1, tiled=True),
    )
    slot_out = slot_out.reshape(slots, model_width).astype(jnp.float32)
    slot_back = slot_back.reshape(slots, model_width).astype(jnp.float32)
    expert_out = slot_out[slot_index].reshape(tok_here, top_count, model_width)
    expert_back = slot_back[slot_index].reshape(tok_here, top_count, model_width)
    mixed = (stem_value + jnp.sum(gates[:, :, None] * expert_out, axis=1)).astype(jnp.bfloat16)
    grad_gates = jnp.sum(upstream[:, None, :] * expert_out, axis=-1)
    _, gate_pull = jax.vjp(gating, picked)
    grad_picked = gate_pull(grad_gates)[0]
    selector = (routes[:, :, None] == jnp.arange(experts, dtype=jnp.int32)).astype(jnp.float32)
    grad_logits = jnp.sum(selector * grad_picked[:, :, None], axis=1)
    grad_normed = jnp.sum(expert_back, axis=1) + jnp.dot(
        grad_logits, router_weight.astype(jnp.float32).T, precision=lax.Precision.HIGHEST
    )
    _, norm_pull = jax.vjp(lambda values: rms_norm(values, norm_gain), stem_value)
    grad_stem = (upstream + norm_pull(grad_normed)[0]).astype(jnp.bfloat16)
    grad_block = with_halo(grad_stem.reshape(rows_here, width, model_width), (("exp", 0),), 1)
    projected = jnp.dot(
        grad_block.reshape(-1, model_width), stem_weight.T, preferred_element_type=jnp.float32
    )
    projected = projected.reshape(rows_here + 2, width, 9, channels)
    shifted = jnp.pad(projected, ((0, 0), (1, 1), (0, 0), (0, 0)))
    terms = [
        shifted[2 - i : 2 - i + rows_here, 2 - j : 2 - j + width, 3 * i + j, :]
        for i in range(3)
        for j in range(3)
    ]
    grad_latent = jnp.sum(jnp.stack(terms, axis=0), axis=0).transpose(0, 2, 1)
    flat_rows = recv_rows.reshape(-1, model_width)
    flat_grads = recv_grads.reshape(-1, model_width)
    dims = (((0,), (0,)), ((), ()))
    term_gate = lax.dot_general(flat_rows, grad_gate_pre, dims, preferred_element_type=jnp.float32)
    term_up = lax.dot_general(flat_rows, grad_up_pre, dims, preferred_element_type=jnp.float32)
    term_down = lax.dot_general(flat_grads, hidden, dims, preferred_element_type=jnp.float32)
    summed = lax.psum_scatter(
        jnp.concatenate([term_gate, term_up, term_down], axis=1).astype(jnp.bfloat16),
        "rep",
        scatter_dimension=0,
        tiled=True,
    ).astype(jnp.float32)
    grad_gate = summed[:, :hid_here]
    grad_up = summed[:, hid_here : 2 * hid_here]
    grad_down = summed[:, 2 * hid_here :].T
    return (mixed, grad_latent, grad_gate, grad_up, grad_down)


def solution(mesh):
    return jax.shard_map(
        local,
        mesh=mesh,
        in_specs=(
            P("exp", None, None),
            P(),
            P(),
            P(),
            P("exp", None),
            P("rep", "exp"),
            P("rep", "exp"),
            P("exp", "rep"),
            P("exp", None),
        ),
        out_specs=(
            P("exp", None),
            P("exp", None, None),
            P("rep", "exp"),
            P("rep", "exp"),
            P("exp", "rep"),
        ),
        check_vma=False,
    )
```

profile of v0, /device:TPU:6, one launch (start us, length us, event | category | flops | bytes accessed | tf_op | source)
XLA Modules:
  0.0 458.4 jit_solution(8518326553651853229)
XLA Ops:
  7.9 11.7 %collective-permute-start.1 = (bf16[1,16,64]{2,1,0:T(8,128)(2,1)S(1)}, bf16[1,16,64]{2,1,0:T(8,128)(2,1)S(1)}, u32[]{:S(2)}, u32[]{:S(2)}) collective-permute-start(bf16[1,16,64]{2,1,0:T(8,128)(2,1)S(1)} %get-tuple-element.55), channel_id=1, source_target_pairs={{8,0},{16,8},{24,16},{32,24},{40,32},{48,40},{56,48},{64,56},{72,6... | collective-permute-start | bytes 6152 | tf_op jit(solution)/shard_map/ppermute | solution.py:19
  19.6 1.9 collective-permute-start
  25.2 2.6 mul.190
  27.7 2.4 mul.191
  32.3 1.4 gather_fusion.2
  34.2 1.3 broadcast_in_dim.17
  35.5 3.0 reshape.269
  38.5 3.4 scatter_custom_fusion
  41.9 2.9 scatter_custom_fusion.1
  46.1 1.3 broadcast_in_dim.18
  47.3 11.0 %all-to-all-start = ((bf16[64,5,1536]{2,1,0:T(8,128)(2,1)}), bf16[64,5,1536]{2,1,0:T(8,128)(2,1)S(1)}, u32[]{:S(2)}, u32[]{:S(2)}) async-start(bf16[64,5,1536]{2,1,0:T(8,128)(2,1)} %bitcast.108), calls=%async_computation | async-start | bytes 3145728 | tf_op jit(solution)/shard_map/all_to_all | solution.py:99
  59.1 74.8 %all-to-all-done = bf16[64,5,1536]{2,1,0:T(8,128)(2,1)S(1)} async-done(((bf16[64,5,1536]{2,1,0:T(8,128)(2,1)}), bf16[64,5,1536]{2,1,0:T(8,128)(2,1)S(1)}, u32[]{:S(2)}, u32[]{:S(2)}) %all-to-all-start) | async-done | bytes 983072 | tf_op jit(solution)/shard_map/all_to_all | solution.py:99
  134.0 1.4 broadcast_in_dim.19
  135.7 7.1 %all-to-all-start.2 = ((bf16[64,5,1536]{2,1,0:T(8,128)(2,1)}), bf16[64,5,1536]{2,1,0:T(8,128)(2,1)}, u32[]{:S(2)}, u32[]{:S(2)}) async-start(bf16[64,5,1536]{2,1,0:T(8,128)(2,1)} %bitcast.107), calls=%async_computation.2 | async-start | bytes 3145728 | tf_op jit(solution)/shard_map/all_to_all | solution.py:114
  144.3 1.6 reshape.226
  145.9 73.0 %all-to-all-done.2 = bf16[64,5,1536]{2,1,0:T(8,128)(2,1)} async-done(((bf16[64,5,1536]{2,1,0:T(8,128)(2,1)}), bf16[64,5,1536]{2,1,0:T(8,128)(2,1)}, u32[]{:S(2)}, u32[]{:S(2)}) %all-to-all-start.2) | async-done | bytes 983072 | tf_op jit(solution)/shard_map/all_to_all | solution.py:114
  218.8 2.4 reshape.232
  221.2 2.7 fusion.42
  223.9 2.7 fusion.43
  226.7 3.4 multiply_convert_fusion.3
  232.3 1.4 reshape.233
  233.7 7.3 %all-to-all-start.3 = ((bf16[64,5,1536]{2,1,0:T(8,128)(2,1)}), bf16[64,5,1536]{2,1,0:T(8,128)(2,1)}, u32[]{:S(2)}, u32[]{:S(2)}) async-start(bf16[64,5,1536]{2,1,0:T(8,128)(2,1)} %reshape.233), calls=%async_computation.3 | async-start | bytes 3145728 | tf_op jit(solution)/shard_map/all_to_all | solution.py:138
  241.0 2.0 convolution_convert_fusion.3
  243.0 1.4 reshape.227
  244.4 2.1 convolution_convert_fusion
  246.5 1.8 convolution_convert_fusion.1
  248.3 1.8 convolution_convert_fusion.2
  250.2 66.9 %all-to-all-done.3 = bf16[64,5,1536]{2,1,0:T(8,128)(2,1)} async-done(((bf16[64,5,1536]{2,1,0:T(8,128)(2,1)}), bf16[64,5,1536]{2,1,0:T(8,128)(2,1)}, u32[]{:S(2)}, u32[]{:S(2)}) %all-to-all-start.3) | async-done | bytes 983072 | tf_op jit(solution)/shard_map/all_to_all | solution.py:138
  317.1 7.1 %all-to-all-start.1 = ((bf16[64,5,1536]{2,1,0:T(8,128)(2,1)}), bf16[64,5,1536]{2,1,0:T(8,128)(2,1)}, u32[]{:S(2)}, u32[]{:S(2)}) async-start(bf16[64,5,1536]{2,1,0:T(8,128)(2,1)} %reshape.227), calls=%async_computation.1 | async-start | bytes 3145728 | tf_op jit(solution)/shard_map/all_to_all | solution.py:113
  324.3 3.2 pad_maximum_fusion
  327.5 5.8 %copy.115 = bf16[1536,1152]{1,0:T(8,128)(2,1)} copy(bf16[1536,1152]{0,1:T(8,128)(2,1)} %pad_maximum_fusion) | data formatting | bytes 7077888
  335.3 1.7 bitcast_reduce_fusion
  337.1 14.1 %all_gather.19 = bf16[8,40,1536]{2,0,1:T(8,128)(2,1)S(1)} all-gather(bf16[8,5,1536]{2,0,1:T(8,128)(2,1)S(1)} %copy.107), channel_id=1, replica_groups=mesh['exp'=64,'rep'=8] {'rep'}, dimensions={1}, use_global_device_ids=true | all-gather | bytes 1105920 | tf_op jit(solution)/shard_map/all_gather | solution.py:147
  351.5 2.3 gather_fusion.1
  353.9 3.1 reshape.235
  356.9 43.4 %all-to-all-done.1 = bf16[64,5,1536]{2,1,0:T(8,128)(2,1)} async-done(((bf16[64,5,1536]{2,1,0:T(8,128)(2,1)}), bf16[64,5,1536]{2,1,0:T(8,128)(2,1)}, u32[]{:S(2)}, u32[]{:S(2)}) %all-to-all-start.1) | async-done | bytes 983072 | tf_op jit(solution)/shard_map/all_to_all | solution.py:113
  400.4 1.7 bitcast_reduce_fusion.1
  402.1 14.5 %all_gather.18 = bf16[8,40,1536]{2,0,1:T(8,128)(2,1)S(1)} all-gather(bf16[8,5,1536]{2,0,1:T(8,128)(2,1)S(1)} %copy.104), channel_id=1, replica_groups=mesh['exp'=64,'rep'=8] {'rep'}, dimensions={1}, use_global_device_ids=true | all-gather | bytes 1105920 | tf_op jit(solution)/shard_map/all_gather | solution.py:146
  416.9 2.4 gather_fusion
  419.3 3.1 reshape.229
  422.4 5.0 %multiply_reduce_fusion = (f32[128,2]{1,0:T(8,128)S(1)}, f32[128,1536]{1,0:T(8,128)}) fusion(f32[128,2,1536]{2,1,0:T(2,128)} %reshape.229, f32[128,1536]{1,0:T(8,128)} %convert_element_type.77, f32[128,2]{1,0:T(8,128)S(1)} %copy.100), kind=kLoop, calls=%fused_computation.18 | loop fusion | flops 1376000 | bytes 3147776 | tf_op jit(solution)/shard_map/reduce_sum | solution.py:154
  427.5 3.0 reduce_sum.177
  430.5 1.9 multiply_reduce_fusion.2
  433.5 1.9 collective-permute-start.3
  435.5 3.9 collective-permute-start.2
  439.4 3.2 collective-permute-done.3
  442.6 4.0 collective-permute-done.2
  447.8 1.2 copy.116
  (121 shorter events, 20.7 us)
Async XLA Ops:
  7.2 23.8 %copy-start = (bf16[144,1536]{1,0:T(8,128)(2,1)S(1)}, bf16[144,1536]{1,0:T(8,128)(2,1)}, u32[]{:S(2)}) copy-start(bf16[144,1536]{1,0:T(8,128)(2,1)} %param.10) | copy-start | bytes 1327108
  7.9 22.5 %collective-permute-start.1 = (bf16[1,16,64]{2,1,0:T(8,128)(2,1)S(1)}, bf16[1,16,64]{2,1,0:T(8,128)(2,1)S(1)}, u32[]{:S(2)}, u32[]{:S(2)}) collective-permute-start(bf16[1,16,64]{2,1,0:T(8,128)(2,1)S(1)} %get-tuple-element.55), channel_id=1, source_target_pairs={{8,0},{16,8},{24,16},{32,24},{40,32},{48,40},{56,48},{64,56},{72,6... | collective-permute-start | bytes 6152 | tf_op jit(solution)/shard_map/ppermute | solution.py:19
  19.6 10.8 %collective-permute-start = (bf16[1,16,64]{2,1,0:T(8,128)(2,1)S(1)}, bf16[1,16,64]{2,1,0:T(8,128)(2,1)S(1)}, u32[]{:S(2)}, u32[]{:S(2)}) collective-permute-start(bf16[1,16,64]{2,1,0:T(8,128)(2,1)S(1)} %get-tuple-element.54), channel_id=1, source_target_pairs={{0,8},{8,16},{16,24},{24,32},{32,40},{40,48},{48,56},{56,64},{64,7... | collective-permute-start | bytes 6152 | tf_op jit(solution)/shard_map/ppermute | solution.py:17
  27.7 2.7 copy-start.13
  30.1 1.8 copy-start.15
  30.1 1.9 copy-start.14
  31.4 0.7 copy-start.19
  31.4 0.5 copy-start.17
  32.3 1.6 copy-start.16
  47.3 86.6 %all-to-all-start = ((bf16[64,5,1536]{2,1,0:T(8,128)(2,1)}), bf16[64,5,1536]{2,1,0:T(8,128)(2,1)S(1)}, u32[]{:S(2)}, u32[]{:S(2)}) async-start(bf16[64,5,1536]{2,1,0:T(8,128)(2,1)} %bitcast.108), calls=%async_computation | async-start | bytes 3145728 | tf_op jit(solution)/shard_map/all_to_all | solution.py:99
  58.4 162.8 %all-gather.4.cloned.1.call-start = ((), (), s32[]{:S(2)}) async-start(), calls=%async_computation.5 | async-start | bytes 1327104 | tf_op jit(solution)/shard_map/all_gather | solution.py:94
  134.0 1.7 copy-start.1
  135.7 83.2 %all-to-all-start.2 = ((bf16[64,5,1536]{2,1,0:T(8,128)(2,1)}), bf16[64,5,1536]{2,1,0:T(8,128)(2,1)}, u32[]{:S(2)}, u32[]{:S(2)}) async-start(bf16[64,5,1536]{2,1,0:T(8,128)(2,1)} %bitcast.107), calls=%async_computation.2 | async-start | bytes 3145728 | tf_op jit(solution)/shard_map/all_to_all | solution.py:114
  142.8 81.2 %all-gather.6.cloned.1.call-start = ((), (), s32[]{:S(2)}) async-start(), calls=%async_computation.6 | async-start | bytes 1327104 | tf_op jit(solution)/shard_map/all_gather | solution.py:95
  143.5 83.1 %all-gather.8.cloned.1.call-start = ((), (), s32[]{:S(2)}) async-start(), calls=%async_computation.7 | async-start | bytes 1327104 | tf_op jit(solution)/shard_map/all_gather | solution.py:97
  226.7 3.4 copy-start.3
  230.1 0.7 copy-start.8
  230.1 0.8 copy-start.10
  230.1 1.4 copy-start.4
  233.7 7.3 %copy-start.12 = (bf16[320,384]{1,0:T(8,128)(2,1)S(1)}, bf16[320,384]{1,0:T(8,128)(2,1)}, u32[]{:S(2)}) copy-start(bf16[320,384]{1,0:T(8,128)(2,1)} %get-tuple-element.47) | copy-start | bytes 737284
  233.7 83.4 %all-to-all-start.3 = ((bf16[64,5,1536]{2,1,0:T(8,128)(2,1)}), bf16[64,5,1536]{2,1,0:T(8,128)(2,1)}, u32[]{:S(2)}, u32[]{:S(2)}) async-start(bf16[64,5,1536]{2,1,0:T(8,128)(2,1)} %reshape.233), calls=%async_computation.3 | async-start | bytes 3145728 | tf_op jit(solution)/shard_map/all_to_all | solution.py:138
  244.4 2.1 copy-start.11
  246.5 1.9 copy-start.9
  317.1 83.3 %all-to-all-start.1 = ((bf16[64,5,1536]{2,1,0:T(8,128)(2,1)}), bf16[64,5,1536]{2,1,0:T(8,128)(2,1)}, u32[]{:S(2)}, u32[]{:S(2)}) async-start(bf16[64,5,1536]{2,1,0:T(8,128)(2,1)} %reshape.227), calls=%async_computation.1 | async-start | bytes 3145728 | tf_op jit(solution)/shard_map/all_to_all | solution.py:113
  324.2 123.6 %reduce-scatter.4.cloned.1.call-start = ((), (), s32[]{:S(2)}) async-start(), calls=%async_computation.8 | async-start | bytes 3981312
  333.3 1.0 copy-start.5
  422.4 5.1 %copy-start.2 = (f32[128,2,1536]{2,1,0:T(2,128)S(1)}, f32[128,2,1536]{2,1,0:T(2,128)}, u32[]{:S(2)}) copy-start(f32[128,2,1536]{2,1,0:T(2,128)} %reshape.235) | copy-start | bytes 4718596
  430.5 1.9 copy-start.20
  430.5 1.9 copy-start.6
  430.5 2.0 copy-start.7
  430.5 2.0 copy-start.18
  433.5 9.0 %collective-permute-start.3 = (bf16[1,64,1536]{2,1,0:T(8,128)(2,1)S(1)}, bf16[1,64,1536]{2,1,0:T(8,128)(2,1)S(1)}, u32[]{:S(2)}, u32[]{:S(2)}) collective-permute-start(bf16[1,64,1536]{2,1,0:T(8,128)(2,1)S(1)} %get-tuple-element.53), channel_id=1, source_target_pairs={{8,0},{16,8},{24,16},{32,24},{40,32},{48,40},{56,48},{64,56},{72,6... | collective-permute-start | bytes 589832 | tf_op jit(solution)/shard_map/ppermute | solution.py:19
  435.5 11.1 %collective-permute-start.2 = (bf16[1,64,1536]{2,1,0:T(8,128)(2,1)S(1)}, bf16[1,64,1536]{2,1,0:T(8,128)(2,1)S(1)}, u32[]{:S(2)}, u32[]{:S(2)}) collective-permute-start(bf16[1,64,1536]{2,1,0:T(8,128)(2,1)S(1)} %get-tuple-element.52), channel_id=1, source_target_pairs={{0,8},{8,16},{16,24},{24,32},{32,40},{40,48},{48,56},{56,64},{64,7... | collective-permute-start | bytes 589832 | tf_op jit(solution)/shard_map/ppermute | solution.py:17
Sparse Core Ops, SparseCore 0:
  61.3 31.8 all-gather.3
  145.7 31.8 all-gather.5
  179.8 31.0 all-gather.7
  333.4 45.9 reduce-scatter.3
where the time goes:
time: 460 us; the launch traced here: 458 us
  waiting for transfers between devices  267 us (58%)
  starting transfers between devices  52.3 us (11%)
  local copies, waits for them, and re-layouts  52.1 us (11%)
  blocking collectives  28.6 us (6%)
  other arithmetic  22.8 us (5%)
  matrix products  21 us (5%)
  between operations  14.3 us (3%)
    all_to_all x1, waiting for transfers between devices, local(): lax.all_to_all(fan_rows, 'exp', split_axis=0, concat_axis=0, tiled=True)  74.8 us
    all_to_all x1, waiting for transfers between devices, local(): lax.all_to_all(fan_grads, 'exp', split_axis=0, concat_axis=0, tiled=True)  73 us
    all_to_all x1, waiting for transfers between devices, local(): lax.all_to_all(back, 'exp', split_axis=0, concat_axis=0, tiled=True)  66.9 us
    all_to_all x1, waiting for transfers between devices, local(): lax.all_to_all(part, 'exp', split_axis=0, concat_axis=0, tiled=True)  43.4 us
    all_gather x1, blocking collectives, local(): lax.all_gather(group_out, 'rep', axis=1, tiled=True)  14.5 us
    all_gather x1, blocking collectives, local(): lax.all_gather(group_back, 'rep', axis=1, tiled=True)  14.1 us
    ppermute x2, starting transfers between devices, with_halo(): lax.ppermute(head, axis, [((i + 1) % count, i) for i in range(ends)])  13.6 us
    unnamed x54, local copies, waits for them, and re-layouts  13.1 us
  transfers between devices with their start and end apart: 12, of which 6 were waited for; matrix products, arithmetic and copies ran while one was open for 14% of the time, Pallas kernels for 0%

commit v1 on v0

--- a/solution.py
+++ b/solution.py
@@ -144,7 +144,9 @@
     ).astype(jnp.bfloat16)
     slot_out, slot_back = (
         lax.all_gather(group_out, "rep", axis=1, tiled=True),
-        lax.all_gather(group_back, "rep", axis=1, tiled=True),
+        jnp.concatenate(
+            lax.all_to_all(jnp.stack([group_back] * lax.axis_size("rep")), "rep", 0, 0), axis=1
+        ),
     )
     slot_out = slot_out.reshape(slots, model_width).astype(jnp.float32)
     slot_back = slot_back.reshape(slots, model_width).astype(jnp.float32)

time: 460 us -> 483 us (1.050)
  waiting for transfers between devices: 267 us -> 289 us
  blocking collectives: 28.6 us -> 22.3 us
    all_to_all x1, waiting for transfers between devices: 43.4 us -> 61.9 us  [local(): lax.all_to_all(part, 'exp', split_axis=0, concat_axis=0, tiled=True)]
    all_gather x1 -> x0, blocking collectives: 14.1 us -> none  [local(): lax.all_gather(group_back, 'rep', axis=1, tiled=True)]
    all_gather x1, blocking collectives: 14.5 us -> 22.3 us  [local(): lax.all_gather(group_out, 'rep', axis=1, tiled=True)]
    unnamed x54 -> x50, local copies, waits for them, and re-layouts: 13.1 us -> 13.1 us
  transfers between devices with their start and end apart: 12 -> 13, of which waited for: 6 -> 6; matrix products, arithmetic and copies ran while one was open for 14% -> 14% of each run, Pallas kernels for 0% -> 0%
where the time goes in v1:
time: 483 us; the launch traced here: 481 us
  waiting for transfers between devices  289 us (60%)
  starting transfers between devices  56.8 us (12%)
  local copies, waits for them, and re-layouts  56 us (12%)
  other arithmetic  22.7 us (5%)
  blocking collectives  22.3 us (5%)
  matrix products  19.9 us (4%)
  between operations  14.3 us (3%)
    all_to_all x1, waiting for transfers between devices, local(): lax.all_to_all(fan_rows, 'exp', split_axis=0, concat_axis=0, tiled=True)  74.8 us
    all_to_all x1, waiting for transfers between devices, local(): lax.all_to_all(fan_grads, 'exp', split_axis=0, concat_axis=0, tiled=True)  73 us
    all_to_all x1, waiting for transfers between devices, local(): lax.all_to_all(back, 'exp', split_axis=0, concat_axis=0, tiled=True)  70.6 us
    all_to_all x1, waiting for transfers between devices, local(): lax.all_to_all(part, 'exp', split_axis=0, concat_axis=0, tiled=True)  61.9 us
    all_gather x1, blocking collectives, local(): lax.all_gather(group_out, 'rep', axis=1, tiled=True)  22.3 us
    ppermute x2, starting transfers between devices, with_halo(): lax.ppermute(head, axis, [((i + 1) % count, i) for i in range(ends)])  13.6 us
    unnamed x50, local copies, waits for them, and re-layouts  13.1 us
    all_to_all x1, starting transfers between devices, local(): lax.all_to_all(fan_rows, 'exp', split_axis=0, concat_axis=0, tiled=True)  11 us
  transfers between devices with their start and end apart: 13, of which 6 were waited for; matrix products, arithmetic and copies ran while one was open for 14% of the time, Pallas kernels for 0%

profile of v1, /device:TPU:6, one launch (start us, length us, event | category | flops | bytes accessed | tf_op | source)
XLA Modules:
  0.0 481.4 jit_solution(4304654060023835509)
XLA Ops:
  7.9 11.7 %collective-permute-start.1 = (bf16[1,16,64]{2,1,0:T(8,128)(2,1)S(1)}, bf16[1,16,64]{2,1,0:T(8,128)(2,1)S(1)}, u32[]{:S(2)}, u32[]{:S(2)}) collective-permute-start(bf16[1,16,64]{2,1,0:T(8,128)(2,1)S(1)} %get-tuple-element.55), channel_id=1, source_target_pairs={{8,0},{16,8},{24,16},{32,24},{40,32},{48,40},{56,48},{64,56},{72,6... | collective-permute-start | bytes 6152 | tf_op jit(solution)/shard_map/ppermute | solution.py:19
  19.6 1.9 collective-permute-start
  25.2 2.6 mul.190
  27.7 2.4 mul.191
  32.3 1.4 gather_fusion.2
  34.2 1.3 broadcast_in_dim.17
  35.5 3.0 reshape.271
  38.5 3.4 scatter_custom_fusion
  41.9 2.9 scatter_custom_fusion.1
  47.3 11.0 %all-to-all-start = ((bf16[64,5,1536]{2,1,0:T(8,128)(2,1)}), bf16[64,5,1536]{2,1,0:T(8,128)(2,1)S(1)}, u32[]{:S(2)}, u32[]{:S(2)}) async-start(bf16[64,5,1536]{2,1,0:T(8,128)(2,1)} %bitcast.108), calls=%async_computation | async-start | bytes 3145728 | tf_op jit(solution)/shard_map/all_to_all | solution.py:99
  59.1 74.8 %all-to-all-done = bf16[64,5,1536]{2,1,0:T(8,128)(2,1)S(1)} async-done(((bf16[64,5,1536]{2,1,0:T(8,128)(2,1)}), bf16[64,5,1536]{2,1,0:T(8,128)(2,1)S(1)}, u32[]{:S(2)}, u32[]{:S(2)}) %all-to-all-start) | async-done | bytes 983072 | tf_op jit(solution)/shard_map/all_to_all | solution.py:99
  134.0 1.4 broadcast_in_dim.19
  135.7 7.1 %all-to-all-start.2 = ((bf16[64,5,1536]{2,1,0:T(8,128)(2,1)}), bf16[64,5,1536]{2,1,0:T(8,128)(2,1)}, u32[]{:S(2)}, u32[]{:S(2)}) async-start(bf16[64,5,1536]{2,1,0:T(8,128)(2,1)} %bitcast.107), calls=%async_computation.2 | async-start | bytes 3145728 | tf_op jit(solution)/shard_map/all_to_all | solution.py:114
  144.3 1.6 reshape.228
  145.9 73.0 %all-to-all-done.2 = bf16[64,5,1536]{2,1,0:T(8,128)(2,1)} async-done(((bf16[64,5,1536]{2,1,0:T(8,128)(2,1)}), bf16[64,5,1536]{2,1,0:T(8,128)(2,1)}, u32[]{:S(2)}, u32[]{:S(2)}) %all-to-all-start.2) | async-done | bytes 983072 | tf_op jit(solution)/shard_map/all_to_all | solution.py:114
  218.8 2.4 reshape.234
  221.2 2.7 fusion.42
  223.9 2.7 fusion.43
  226.7 3.4 multiply_convert_fusion.3
  232.3 1.4 reshape.235
  233.6 7.3 %all-to-all-start.3 = ((bf16[64,5,1536]{2,1,0:T(8,128)(2,1)}), bf16[64,5,1536]{2,1,0:T(8,128)(2,1)}, u32[]{:S(2)}, u32[]{:S(2)}) async-start(bf16[64,5,1536]{2,1,0:T(8,128)(2,1)} %reshape.235), calls=%async_computation.3 | async-start | bytes 3145728 | tf_op jit(solution)/shard_map/all_to_all | solution.py:138
  240.9 2.0 convolution_convert_fusion.3
  242.9 1.4 reshape.229
  244.3 2.0 convolution_convert_fusion
  246.4 70.6 %all-to-all-done.3 = bf16[64,5,1536]{2,1,0:T(8,128)(2,1)} async-done(((bf16[64,5,1536]{2,1,0:T(8,128)(2,1)}), bf16[64,5,1536]{2,1,0:T(8,128)(2,1)}, u32[]{:S(2)}, u32[]{:S(2)}) %all-to-all-start.3) | async-done | bytes 983072 | tf_op jit(solution)/shard_map/all_to_all | solution.py:138
  317.0 7.1 %all-to-all-start.1 = ((bf16[64,5,1536]{2,1,0:T(8,128)(2,1)}), bf16[64,5,1536]{2,1,0:T(8,128)(2,1)}, u32[]{:S(2)}, u32[]{:S(2)}) async-start(bf16[64,5,1536]{2,1,0:T(8,128)(2,1)} %reshape.229), calls=%async_computation.1 | async-start | bytes 3145728 | tf_op jit(solution)/shard_map/all_to_all | solution.py:113
  324.2 1.8 convolution_convert_fusion.1
  326.9 2.0 pad_maximum_fusion
  328.8 5.8 %copy.115 = bf16[1536,1152]{1,0:T(8,128)(2,1)} copy(bf16[1536,1152]{0,1:T(8,128)(2,1)} %pad_maximum_fusion) | data formatting | bytes 7077888
  336.7 1.7 bitcast_reduce_fusion
  338.4 61.9 %all-to-all-done.1 = bf16[64,5,1536]{2,1,0:T(8,128)(2,1)} async-done(((bf16[64,5,1536]{2,1,0:T(8,128)(2,1)}), bf16[64,5,1536]{2,1,0:T(8,128)(2,1)}, u32[]{:S(2)}, u32[]{:S(2)}) %all-to-all-start.1) | async-done | bytes 983072 | tf_op jit(solution)/shard_map/all_to_all | solution.py:113
  401.3 4.5 all-to-all-start.4
  405.8 1.7 bitcast_reduce_fusion.1
  407.6 22.3 %all_gather.15 = bf16[8,40,1536]{2,0,1:T(8,128)(2,1)S(1)} all-gather(bf16[8,5,1536]{2,0,1:T(8,128)(2,1)S(1)} %copy.104), channel_id=1, replica_groups=mesh['exp'=64,'rep'=8] {'rep'}, dimensions={1}, use_global_device_ids=true | all-gather | bytes 1105920 | tf_op jit(solution)/shard_map/all_gather | solution.py:146
  430.2 2.4 gather_fusion
  432.5 2.2 reshape.231
  434.8 4.6 multiply_reduce_fusion
  439.6 1.4 convert_bitcast_fusion
  441.0 2.9 copy.108
  443.9 2.1 reshape.240
  445.9 2.3 gather_fusion.1
  448.3 2.2 reshape.237
  450.5 3.0 reduce_sum.177
  453.5 1.9 multiply_reduce_fusion.2
  456.5 1.9 collective-permute-start.3
  458.4 3.9 collective-permute-start.2
  462.4 3.2 collective-permute-done.3
  465.6 4.0 collective-permute-done.2
  (121 shorter events, 24.7 us)
Async XLA Ops:
  7.2 23.8 %copy-start = (bf16[144,1536]{1,0:T(8,128)(2,1)S(1)}, bf16[144,1536]{1,0:T(8,128)(2,1)}, u32[]{:S(2)}) copy-start(bf16[144,1536]{1,0:T(8,128)(2,1)} %param.10) | copy-start | bytes 1327108
  7.9 22.5 %collective-permute-start.1 = (bf16[1,16,64]{2,1,0:T(8,128)(2,1)S(1)}, bf16[1,16,64]{2,1,0:T(8,128)(2,1)S(1)}, u32[]{:S(2)}, u32[]{:S(2)}) collective-permute-start(bf16[1,16,64]{2,1,0:T(8,128)(2,1)S(1)} %get-tuple-element.55), channel_id=1, source_target_pairs={{8,0},{16,8},{24,16},{32,24},{40,32},{48,40},{56,48},{64,56},{72,6... | collective-permute-start | bytes 6152 | tf_op jit(solution)/shard_map/ppermute | solution.py:19
  19.6 10.8 %collective-permute-start = (bf16[1,16,64]{2,1,0:T(8,128)(2,1)S(1)}, bf16[1,16,64]{2,1,0:T(8,128)(2,1)S(1)}, u32[]{:S(2)}, u32[]{:S(2)}) collective-permute-start(bf16[1,16,64]{2,1,0:T(8,128)(2,1)S(1)} %get-tuple-element.54), channel_id=1, source_target_pairs={{0,8},{8,16},{16,24},{24,32},{32,40},{40,48},{48,56},{56,64},{64,7... | collective-permute-start | bytes 6152 | tf_op jit(solution)/shard_map/ppermute | solution.py:17
  27.7 2.7 copy-start.11
  30.1 1.8 copy-start.13
  30.1 1.9 copy-start.12
  31.4 0.7 copy-start.17
  31.4 0.5 copy-start.15
  32.3 1.6 copy-start.14
  47.3 86.6 %all-to-all-start = ((bf16[64,5,1536]{2,1,0:T(8,128)(2,1)}), bf16[64,5,1536]{2,1,0:T(8,128)(2,1)S(1)}, u32[]{:S(2)}, u32[]{:S(2)}) async-start(bf16[64,5,1536]{2,1,0:T(8,128)(2,1)} %bitcast.108), calls=%async_computation | async-start | bytes 3145728 | tf_op jit(solution)/shard_map/all_to_all | solution.py:99
  58.4 162.8 %all-gather.4.cloned.1.call-start = ((), (), s32[]{:S(2)}) async-start(), calls=%async_computation.6 | async-start | bytes 1327104 | tf_op jit(solution)/shard_map/all_gather | solution.py:94
  134.0 1.7 copy-start.1
  135.7 83.2 %all-to-all-start.2 = ((bf16[64,5,1536]{2,1,0:T(8,128)(2,1)}), bf16[64,5,1536]{2,1,0:T(8,128)(2,1)}, u32[]{:S(2)}, u32[]{:S(2)}) async-start(bf16[64,5,1536]{2,1,0:T(8,128)(2,1)} %bitcast.107), calls=%async_computation.2 | async-start | bytes 3145728 | tf_op jit(solution)/shard_map/all_to_all | solution.py:114
  142.8 81.2 %all-gather.6.cloned.1.call-start = ((), (), s32[]{:S(2)}) async-start(), calls=%async_computation.7 | async-start | bytes 1327104 | tf_op jit(solution)/shard_map/all_gather | solution.py:95
  143.5 83.1 %all-gather.8.cloned.1.call-start = ((), (), s32[]{:S(2)}) async-start(), calls=%async_computation.8 | async-start | bytes 1327104 | tf_op jit(solution)/shard_map/all_gather | solution.py:97
  226.7 3.4 copy-start.2
  230.1 0.7 copy-start.7
  230.1 0.8 copy-start.9
  230.1 1.4 copy-start.3
  233.6 7.3 %copy-start.10 = (bf16[320,384]{1,0:T(8,128)(2,1)S(1)}, bf16[320,384]{1,0:T(8,128)(2,1)}, u32[]{:S(2)}) copy-start(bf16[320,384]{1,0:T(8,128)(2,1)} %get-tuple-element.47) | copy-start | bytes 737284
  233.6 83.4 %all-to-all-start.3 = ((bf16[64,5,1536]{2,1,0:T(8,128)(2,1)}), bf16[64,5,1536]{2,1,0:T(8,128)(2,1)}, u32[]{:S(2)}, u32[]{:S(2)}) async-start(bf16[64,5,1536]{2,1,0:T(8,128)(2,1)} %reshape.235), calls=%async_computation.3 | async-start | bytes 3145728 | tf_op jit(solution)/shard_map/all_to_all | solution.py:138
  317.0 83.3 %all-to-all-start.1 = ((bf16[64,5,1536]{2,1,0:T(8,128)(2,1)}), bf16[64,5,1536]{2,1,0:T(8,128)(2,1)}, u32[]{:S(2)}, u32[]{:S(2)}) async-start(bf16[64,5,1536]{2,1,0:T(8,128)(2,1)} %reshape.229), calls=%async_computation.1 | async-start | bytes 3145728 | tf_op jit(solution)/shard_map/all_to_all | solution.py:113
  324.2 146.7 %reduce-scatter.4.cloned.1.call-start = ((), (), s32[]{:S(2)}) async-start(), calls=%async_computation.9 | async-start | bytes 3981312
  324.2 1.8 copy-start.8
  334.6 1.0 copy-start.4
  401.3 38.2 %all-to-all-start.4 = ((bf16[8,8,5,1536]{3,1,2,0:T(8,128)(2,1)}), bf16[8,8,5,1536]{3,1,2,0:T(8,128)(2,1)}, u32[]{:S(2)}, u32[]{:S(2)}) async-start(bf16[8,8,5,1536]{3,1,2,0:T(8,128)(2,1)} %stack.52), calls=%async_computation.4 | async-start | bytes 1966080 | tf_op jit(solution)/shard_map/all_to_all | solution.py:148
  453.5 1.9 copy-start.18
  453.5 1.9 copy-start.5
  453.5 1.9 copy-start.6
  453.5 1.9 copy-start.16
  456.5 9.1 %collective-permute-start.3 = (bf16[1,64,1536]{2,1,0:T(8,128)(2,1)S(1)}, bf16[1,64,1536]{2,1,0:T(8,128)(2,1)S(1)}, u32[]{:S(2)}, u32[]{:S(2)}) collective-permute-start(bf16[1,64,1536]{2,1,0:T(8,128)(2,1)S(1)} %get-tuple-element.53), channel_id=1, source_target_pairs={{8,0},{16,8},{24,16},{32,24},{40,32},{48,40},{56,48},{64,56},{72,6... | collective-permute-start | bytes 589832 | tf_op jit(solution)/shard_map/ppermute | solution.py:19
  458.4 11.2 %collective-permute-start.2 = (bf16[1,64,1536]{2,1,0:T(8,128)(2,1)S(1)}, bf16[1,64,1536]{2,1,0:T(8,128)(2,1)S(1)}, u32[]{:S(2)}, u32[]{:S(2)}) collective-permute-start(bf16[1,64,1536]{2,1,0:T(8,128)(2,1)S(1)} %get-tuple-element.52), channel_id=1, source_target_pairs={{0,8},{8,16},{16,24},{24,32},{32,40},{40,48},{48,56},{56,64},{64,7... | collective-permute-start | bytes 589832 | tf_op jit(solution)/shard_map/ppermute | solution.py:17
Sparse Core Ops, SparseCore 0:
  61.3 31.8 all-gather.3
  145.7 31.8 all-gather.5
  179.8 31.0 all-gather.7
  334.8 45.9 reduce-scatter.3
